TPU v7x, 512 devices: a whole 4x8x8 slice. The times are simulated.
512 devices in a mesh: dp: 32 (over z, x), tensor: 16 (over y, core).
Axes of the slice: x: 4, y: 8, z: 8, core: 2. Of those that a mesh axis runs over, the one named last changes fastest.
Arguments:
- tokens: int32 [64, 4], P('dp'), may hold values from 0 to 77823
- embed_table: bfloat16 [77824, 3584], P('dp', 'tensor'), may hold values from -6 to 6
- norm_gain: bfloat16 [3584], P('tensor'), may hold values from 0.099609375 to 1.8984375
- w_query: bfloat16 [3584, 2048], P('tensor'), may hold values from -0.09375 to 0.09375
- w_key_value: bfloat16 [3584, 1024], P('tensor'), may hold values from -0.09375 to 0.09375
- cache_keys: bfloat16 [64, 4, 64, 128], P('dp'), may hold values from -6 to 6
- cache_values: bfloat16 [64, 4, 64, 128], P('dp'), may hold values from -6 to 6
- cache_len: int32 [64], P('dp'), may hold values from 1 to 64, 2048 in all
- teacher_rows: bfloat16 [512, 8192], P('dp', 'tensor'), may hold values from -6 to 6
- w_llama: bfloat16 [8192, 2, 14336], P('tensor', None, 'dp'), may hold values from -0.0625 to 0.0625
- w_qwen: bfloat16 [8192, 2, 14784], P('tensor', None, 'dp'), may hold values from -0.0625 to 0.0625
- rollout_len: int32 [32, 4], P('dp'), may hold values from 1 to 8, 16 in all within a row
- teacher_of: int32 [32, 4], P('dp'), may hold values from 0 to 1
Outputs:
- attn_out: bfloat16 [64, 4, 2048], P('dp', None, 'tensor')
- llama_hidden: bfloat16 [512, 14336], P('tensor', 'dp')
- qwen_hidden: bfloat16 [512, 14784], P('tensor', 'dp')
Inputs may be any that keep to these rules, and one draw needn't show every extreme that they name: `cache_len`: at least one rollout fills all 64 slots. `rollout_len`: each row sums to 16; the longest rollout of a row has 8 token rows.
All inputs are finite; a program needn't handle non-finite values. No bound on the sum of `cache_len` on one device may be relied on, other than what follows from the above.
Results may differ from a plain program's by a relative error of at most 0.01.
Values may be sent and summed in bfloat16 or wider, within the bound.
No kernel may reach another device: no remote copies, remote signals or barrier semaphores. Data moves between devices by JAX's collectives and lax.ppermute only.
A program may use at most 64 MiB of HBM per device.

v0:
```python
import math
import jax
import jax.numpy as jnp
from jax import lax
from jax.sharding import PartitionSpec as P

DS = 3584
HEADS = 16
KVH = 4
HD = 128
TT_DEV = 16


def row_owner(rollout_len, teacher_of, per_group):
    ends = jnp.cumsum(rollout_len, axis=1)
    offset = jnp.arange(per_group, dtype=jnp.int32)
    which = jnp.sum((offset[None, :, None] >= ends[:, None, :]).astype(jnp.int32), axis=2)
    slots = jnp.arange(rollout_len.shape[1], dtype=jnp.int32)
    pick = (which[:, :, None] == slots[None, None, :]).astype(jnp.int32)
    return jnp.sum(pick * teacher_of[:, None, :], axis=2).reshape(-1)


def attend(query, keys_cache, values_cache, keys_new, values_new, cache_len):
    scale = 1.0 / math.sqrt(query.shape[-1])
    query_f = query.astype(jnp.float32)
    score_cache = jnp.einsum("bshd,bhld->bshl", query_f, keys_cache.astype(jnp.float32)) * scale
    score_new = jnp.einsum("bshd,bthd->bsht", query_f, keys_new.astype(jnp.float32)) * scale
    live = jnp.arange(keys_cache.shape[2], dtype=jnp.int32)[None, :] < cache_len[:, None]
    steps = query.shape[1]
    causal = jnp.arange(steps)[:, None] >= jnp.arange(steps)[None, :]
    score_cache = jnp.where(live[:, None, None, :], score_cache, -jnp.inf)
    score_new = jnp.where(causal[None, :, None, :], score_new, -jnp.inf)
    top = jnp.maximum(jnp.max(score_cache, axis=3), jnp.max(score_new, axis=3))[..., None]
    exp_cache = jnp.exp(score_cache - top)
    exp_new = jnp.exp(score_new - top)
    total = jnp.sum(exp_cache, axis=3, keepdims=True) + jnp.sum(exp_new, axis=3, keepdims=True)
    prob_cache = (exp_cache / total).astype(jnp.bfloat16)
    prob_new = (exp_new / total).astype(jnp.bfloat16)
    mixed = jnp.einsum(
        "bshl,bhld->bshd", prob_cache.astype(jnp.float32), values_cache.astype(jnp.float32)
    )
    mixed = mixed + jnp.einsum(
        "bsht,bthd->bshd", prob_new.astype(jnp.float32), values_new.astype(jnp.float32)
    )
    return mixed.astype(jnp.bfloat16)


def shards(
    tokens,
    embed_table,
    norm_gain,
    w_query,
    w_key_value,
    cache_keys,
    cache_values,
    cache_len,
    teacher_rows,
    w_llama,
    w_qwen,
    rollout_len,
    teacher_of,
):
    all_tokens, all_lengths, all_owners = (
        lax.all_gather(tokens, "dp", axis=0, tiled=True),
        lax.all_gather(rollout_len, "dp", axis=0, tiled=True),
        lax.all_gather(teacher_of, "dp", axis=0, tiled=True),
    )
    table_rows = embed_table.shape[0]
    local_id = all_tokens - lax.axis_index("dp") * table_rows
    inside = jnp.logical_and(local_id >= 0, local_id < table_rows)
    picked = jnp.take(embed_table, jnp.clip(local_id, 0, table_rows - 1), axis=0)
    term = jnp.where(inside[:, :, None], picked.astype(jnp.float32), 0.0)
    embedded = lax.psum_scatter(term, "dp", scatter_dimension=0, tiled=True).astype(jnp.bfloat16)
    rollouts, steps, columns = embedded.shape
    x_float = embedded.astype(jnp.float32)
    scaled = (x_float * norm_gain.astype(jnp.float32)).astype(jnp.bfloat16).reshape(-1, columns)
    query_part = jnp.dot(scaled, w_query, preferred_element_type=jnp.float32)
    pair_part = jnp.dot(scaled, w_key_value, preferred_element_type=jnp.float32)
    squares = jnp.sum(x_float * x_float, axis=2).reshape(-1)
    heads_here = HEADS // lax.axis_size("tensor")
    head_first = lax.axis_index("tensor") * heads_here
    query_sum, pair_sum, square_sum = lax.psum((query_part, pair_part, squares), "tensor")
    query_own = lax.dynamic_slice_in_dim(query_sum, head_first * HD, heads_here * HD, 1)
    inverse = lax.rsqrt(square_sum / DS + 1e-06)[:, None]
    query = (query_own * inverse).astype(jnp.bfloat16).reshape(rollouts, steps, heads_here, HD)
    key_value = (pair_sum * inverse).astype(jnp.bfloat16).reshape(rollouts, steps, 2, KVH, HD)
    kv_index = (head_first + jnp.arange(heads_here, dtype=jnp.int32)) // (HEADS // KVH)
    keys_cache = jnp.take(cache_keys, kv_index, axis=1)
    values_cache = jnp.take(cache_values, kv_index, axis=1)
    keys_new = jnp.take(key_value[:, :, 0], kv_index, axis=2)
    values_new = jnp.take(key_value[:, :, 1], kv_index, axis=2)
    attn_out = attend(query, keys_cache, values_cache, keys_new, values_new, cache_len).reshape(
        rollouts, steps, heads_here * HD
    )
    llama_cols = w_llama.shape[2]
    qwen_cols = w_qwen.shape[2]
    llama_flat = w_llama.reshape(w_llama.shape[0], 2 * llama_cols)
    qwen_flat = w_qwen.reshape(w_qwen.shape[0], 2 * qwen_cols)
    piece = lax.all_gather(teacher_rows, "dp", axis=0, tiled=True)
    first_part = jnp.dot(piece, llama_flat, preferred_element_type=jnp.float32)
    second_part = jnp.dot(piece, qwen_flat, preferred_element_type=jnp.float32)
    partial_rows = jnp.concatenate([first_part, second_part], axis=1)
    rows_here = partial_rows.shape[0] // lax.axis_size("tensor")
    row_first = lax.axis_index("tensor") * rows_here
    summed_all = lax.psum(partial_rows, "tensor")
    summed = lax.dynamic_slice_in_dim(summed_all, row_first, rows_here, 0)
    owner_all = row_owner(all_lengths, all_owners, TT_DEV)
    owner = lax.dynamic_slice_in_dim(owner_all, row_first, rows_here, 0)
    gate_llama = summed[:, :llama_cols]
    up_llama = summed[:, llama_cols : 2 * llama_cols]
    gate_qwen = summed[:, 2 * llama_cols : 2 * llama_cols + qwen_cols]
    up_qwen = summed[:, 2 * llama_cols + qwen_cols :]
    llama_hidden = jnp.where((owner == 0)[:, None], jax.nn.silu(gate_llama) * up_llama, 0.0).astype(
        jnp.bfloat16
    )
    qwen_hidden = jnp.where((owner == 1)[:, None], jax.nn.silu(gate_qwen) * up_qwen, 0.0).astype(
        jnp.bfloat16
    )
    return (attn_out, llama_hidden, qwen_hidden)


def solution(mesh):
    return jax.shard_map(
        shards,
        mesh=mesh,
        in_specs=(
            P("dp", None),
            P("dp", "tensor"),
            P("tensor"),
            P("tensor", None),
            P("tensor", None),
            P("dp", None, None, None),
            P("dp", None, None, None),
            P("dp"),
            P("dp", "tensor"),
            P("tensor", None, "dp"),
            P("tensor", None, "dp"),
            P("dp", None),
            P("dp", None),
        ),
        out_specs=(P("dp", None, "tensor"), P("tensor", "dp"), P("tensor", "dp")),
        check_vma=False,
    )
```

profile of v0, /device:TPU:1, one launch (start us, length us, event | category | flops | bytes accessed | tf_op | source)
XLA Modules:
  0.0 396.1 jit_solution(5077311815255898789)
XLA Ops:
  7.2 40.1 %all-gather = s32[32,2,4]{2,1,0:T(2,128)S(1)} all-gather(s32[1,2,4]{2,1,0:T(2,128)} %bitcast.99), channel_id=1, replica_groups=mesh['dp'=32,'tensor'=16] {'dp'}, dimensions={0}, use_global_device_ids=true | all-gather | bytes 1056 | tf_op jit(solution)/shard_map/all_gather | solution.py:64
  47.6 1.9 copy.98
  49.6 1.2 gather_fusion
  51.2 114.2 %all-reduce.7 = bf16[64,4,224]{2,1,0:T(4,128)(2,1)S(1)} all-reduce(f32[64,4,224]{2,1,0:T(4,128)S(1)} %convert_select_fusion), channel_id=2, replica_groups=mesh['dp'=32,'tensor'=16] {'dp'}, use_global_device_ids=true, to_apply=%region_0.2.clone | all-reduce | flops 57344 | bytes 344064
  165.4 1.3 dynamic-slice.14
  167.4 35.3 %all_gather.15 = bf16[512,512]{1,0:T(8,128)(2,1)S(1)} all-gather(bf16[16,512]{1,0:T(8,128)(2,1)S(1)} %copy-done.3), channel_id=1, replica_groups=mesh['dp'=32,'tensor'=16] {'dp'}, dimensions={0}, use_global_device_ids=true | all-gather | bytes 540672 | tf_op jit(solution)/shard_map/all_gather | solution.py:99
  202.7 1.3 copy.105
  204.3 0.7 fusion.53
  205.0 0.7 fusion.52
  206.1 0.8 fusion.50
  207.0 2.2 pad_maximum_fusion
  209.3 1.0 copy-done.2
  210.5 92.0 %all-reduce.1 = (f32[8]{0:T(128)S(1)}, f32[8,1024]{1,0:T(8,128)S(1)}) all-reduce(f32[8]{0:T(128)S(1)} %reshape.171, f32[8,1024]{1,0:T(8,128)S(1)} %fusion.51), channel_id=1, replica_groups=mesh['dp'=32,'tensor'=16] {'tensor'}, use_global_device_ids=true, to_apply=%region_3.5 | all-reduce | flops 8200 | bytes 65600 | tf_op jit(solution)/shard_map/psum | solution.py:82
  302.5 31.4 %all-gather.2 = s32[32,1,4]{2,1,0:T(1,128)S(1)} all-gather(s32[1,1,4]{2,1,0:T(1,128)S(1)} %bitcast.100), channel_id=1, replica_groups=mesh['dp'=32,'tensor'=16] {'dp'}, dimensions={0}, use_global_device_ids=true | all-gather | bytes 528 | tf_op jit(solution)/shard_map/all_gather | solution.py:66
  334.0 30.2 %all-gather.1 = s32[32,1,4]{2,1,0:T(1,128)S(1)} all-gather(s32[1,1,4]{2,1,0:T(1,128)S(1)} %bitcast.101), channel_id=1, replica_groups=mesh['dp'=32,'tensor'=16] {'dp'}, dimensions={0}, use_global_device_ids=true | all-gather | bytes 528 | tf_op jit(solution)/shard_map/all_gather | solution.py:65
  364.8 16.7 %all-reduce.6.cloned.1.call-done = (f32[8,2048]{1,0:T(8,128)}, f32[512,1820]{0,1:T(8,128)}) async-done(((f32[8,2048]{1,0:T(8,128)}, f32[512,1820]{0,1:T(8,128)}), (f32[8,2048]{1,0:T(8,128)}, f32[512,1820]{0,1:T(8,128)})) %all-reduce.6.cloned.1.call-update) | async-done | bytes 3792912 | tf_op jit(solution)/shard_map/psum | solution.py:82
  381.5 0.8 multiply_convert_fusion.1
  382.3 1.0 fusion.48
  383.6 1.2 fusion.10
  384.8 0.7 copy.107
  385.5 1.3 fusion.8
  386.8 0.7 copy.108
  387.5 0.9 fusion.14
  388.5 0.8 fusion.5
  (53 shorter events, 2.9 us)
Async XLA Ops:
  7.2 197.8 %copy-start = (bf16[512,2,448]{0,2,1:T(8,128)(2,1)S(1)}, bf16[512,2,448]{0,2,1:T(8,128)(2,1)}, u32[]{:S(2)}) copy-start(bf16[512,2,448]{0,2,1:T(8,128)(2,1)} %param.26) | copy-start | bytes 2752516
  7.2 374.3 %all-reduce.6.cloned.1.call-start = ((), (), s32[]{:S(2)}) async-start(), calls=%async_computation | async-start | bytes 7602176 | tf_op jit(solution)/shard_map/psum | solution.py:82
  47.6 117.8 %copy-start.6 = (bf16[224]{0:T(256)(128)(2,1)S(1)}, bf16[224]{0:T(256)(128)(2,1)}, u32[]{:S(2)}) copy-start(bf16[224]{0:T(256)(128)(2,1)} %param.19) | copy-start | bytes 1348
  47.6 119.8 %copy-start.3 = (bf16[16,512]{1,0:T(8,128)(2,1)S(1)}, bf16[16,512]{1,0:T(8,128)(2,1)}, u32[]{:S(2)}) copy-start(bf16[16,512]{1,0:T(8,128)(2,1)} %param.25) | copy-start | bytes 49156
  205.0 1.2 copy-start.1
  209.2 1.0 copy-start.2
  209.2 93.3 %copy-start.4 = (s32[1,4]{1,0:T(1,128)S(1)}, s32[1,4]{1,0:T(1,128)}, u32[]{:S(2)}) copy-start(s32[1,4]{1,0:T(1,128)} %param.29) | copy-start | bytes 52
  209.2 124.8 %copy-start.5 = (s32[1,4]{1,0:T(1,128)S(1)}, s32[1,4]{1,0:T(1,128)}, u32[]{:S(2)}) copy-start(s32[1,4]{1,0:T(1,128)} %param.28) | copy-start | bytes 52
  209.2 155.4 %copy-start.7 = (s32[2]{0:T(128)S(1)}, s32[2]{0:T(128)}, u32[]{:S(2)}) copy-start(s32[2]{0:T(128)} %param.24) | copy-start | bytes 28
Sparse Core Ops, SparseCore 0:
  209.4 172.0 all-reduce.5
where the time goes:
time: 397 us; the launch traced here: 396 us
  blocking collectives  343 us (86%)
  waiting for transfers between devices  16.7 us (4%)
  between operations  14.9 us (4%)
  local copies, waits for them, and re-layouts  9.69 us (2%)
  other arithmetic  6.34 us (2%)
  matrix products  5.2 us (1%)
    unnamed x1, blocking collectives  114 us
    psum x1, blocking collectives, shards(): lax.psum((query_part, pair_part, squares), 'tensor')  92 us
    all_gather x1, blocking collectives, shards(): lax.all_gather(tokens, 'dp', axis=0, tiled=True)  40.1 us
    all_gather x1, blocking collectives, shards(): piece = lax.all_gather(teacher_rows, 'dp', axis=0, tiled=True)  35.3 us
    all_gather x1, blocking collectives, shards(): lax.all_gather(teacher_of, 'dp', axis=0, tiled=True)  31.4 us
    all_gather x1, blocking collectives, shards(): lax.all_gather(rollout_len, 'dp', axis=0, tiled=True)  30.2 us
    psum x1, waiting for transfers between devices, shards(): lax.psum((query_part, pair_part, squares), 'tensor')  16.7 us
  transfers between devices with their start and end apart: 1, of which 1 were waited for; matrix products, arithmetic and copies ran while one was open for 0% of the time, Pallas kernels for 0%

commit v1 on v0

--- a/solution.py
+++ b/solution.py
@@ -60,8 +60,17 @@
     rollout_len,
     teacher_of,
 ):
+
+    def sections_list(view):
+        return jnp.concatenate(
+            lax.all_to_all(
+                jnp.stack(lax.axis_size("dp") * [view]), "dp", concat_axis=0, split_axis=0
+            ),
+            0,
+        )
+
     all_tokens, all_lengths, all_owners = (
-        lax.all_gather(tokens, "dp", axis=0, tiled=True),
+        sections_list(tokens),
         lax.all_gather(rollout_len, "dp", axis=0, tiled=True),
         lax.all_gather(teacher_of, "dp", axis=0, tiled=True),
     )

time: 397 us -> 364 us (0.917)
  blocking collectives: 343 us -> 310 us
  starting transfers between devices: 0.04 us -> 13.7 us
  waiting for transfers between devices: 16.7 us -> 4.23 us
    all_gather x1 -> x0, blocking collectives: 40.1 us -> none  [shards(): lax.all_gather(tokens, 'dp', axis=0, tiled=True)]
    all_to_all x0 -> x1, starting transfers between devices: none -> 13.7 us  [sections_list(): lax.all_to_all(jnp.stack(lax.axis_size('dp') * [view]), 'dp', concat_axis...]
    psum x1, waiting for transfers between devices: 16.7 us -> 4.21 us  [shards(): lax.psum((query_part, pair_part, squares), 'tensor')]
    psum x1, blocking collectives: 92 us -> 98.2 us  [shards(): lax.psum((query_part, pair_part, squares), 'tensor')]
  transfers between devices with their start and end apart: 1 -> 2, of which waited for: 1 -> 1; matrix products, arithmetic and copies ran while one was open for 0% -> 2% of each run, Pallas kernels for 0% -> 0%
where the time goes in v1:
time: 364 us
  blocking collectives  310 us (85%)
  between operations  14.9 us (4%)
  starting transfers between devices  13.7 us (4%)
  local copies, waits for them, and re-layouts  9.34 us (3%)
  other arithmetic  6.34 us (2%)
  matrix products  5.21 us (1%)
  waiting for transfers between devices  4.23 us (1%)
    unnamed x1, blocking collectives  114 us
    psum x1, blocking collectives, shards(): lax.psum((query_part, pair_part, squares), 'tensor')  98.2 us
    all_gather x1, blocking collectives, shards(): piece = lax.all_gather(teacher_rows, 'dp', axis=0, tiled=True)  38.6 us
    all_gather x1, blocking collectives, shards(): lax.all_gather(rollout_len, 'dp', axis=0, tiled=True)  29.4 us
    all_gather x1, blocking collectives, shards(): lax.all_gather(teacher_of, 'dp', axis=0, tiled=True)  29.3 us
    all_to_all x1, starting transfers between devices, sections_list(): lax.all_to_all(jnp.stack(lax.axis_size('dp') * [view]), 'dp', concat_axis...  13.7 us
  transfers between devices with their start and end apart: 2, of which 1 were waited for; matrix products, arithmetic and copies ran while one was open for 2% of the time, Pallas kernels for 0%

profile of v1, /device:TPU:1, one launch (start us, length us, event | category | flops | bytes accessed | tf_op | source)
XLA Modules:
  0.0 363.5 jit_solution(8620308361183107889)
XLA Ops:
  7.2 1.4 stack.2
  8.6 13.7 %all-to-all-start = ((s32[32,2,4]{2,1,0:T(2,128)}), s32[32,2,4]{2,1,0:T(2,128)S(1)}, u32[]{:S(2)}, u32[]{:S(2)}) async-start(s32[32,2,4]{2,1,0:T(2,128)} %stack.2), calls=%async_computation | async-start | bytes 65536 | tf_op jit(solution)/shard_map/all_to_all | solution.py:66
  22.3 38.6 %all_gather.11 = bf16[512,512]{1,0:T(8,128)(2,1)S(1)} all-gather(bf16[16,512]{1,0:T(8,128)(2,1)} %param.25), channel_id=1, replica_groups=mesh['dp'=32,'tensor'=16] {'dp'}, dimensions={0}, use_global_device_ids=true | all-gather | bytes 540672 | tf_op jit(solution)/shard_map/all_gather | solution.py:108
  61.0 1.3 copy.143
  62.5 0.7 fusion.53
  63.2 0.7 fusion.52
  63.9 2.2 pad_maximum_fusion
  66.1 1.0 copy.136
  67.2 1.3 dynamic-slice.14
  69.5 1.2 gather_fusion
  71.1 114.3 %all-reduce.7 = bf16[64,4,224]{2,1,0:T(4,128)(2,1)S(1)} all-reduce(f32[64,4,224]{2,1,0:T(4,128)S(1)} %convert_select_fusion), channel_id=2, replica_groups=mesh['dp'=32,'tensor'=16] {'dp'}, use_global_device_ids=true, to_apply=%region_0.2.clone | all-reduce | flops 57344 | bytes 344064
  185.5 0.9 fusion.50
  187.0 29.3 %all-gather.1 = s32[32,1,4]{2,1,0:T(1,128)S(1)} all-gather(s32[1,1,4]{2,1,0:T(1,128)S(1)} %bitcast.101), channel_id=1, replica_groups=mesh['dp'=32,'tensor'=16] {'dp'}, dimensions={0}, use_global_device_ids=true | all-gather | bytes 528 | tf_op jit(solution)/shard_map/all_gather | solution.py:75
  216.4 29.4 %all-gather = s32[32,1,4]{2,1,0:T(1,128)S(1)} all-gather(s32[1,1,4]{2,1,0:T(1,128)S(1)} %bitcast.102), channel_id=1, replica_groups=mesh['dp'=32,'tensor'=16] {'dp'}, dimensions={0}, use_global_device_ids=true | all-gather | bytes 528 | tf_op jit(solution)/shard_map/all_gather | solution.py:74
  246.5 98.2 %all-reduce.1 = (f32[8]{0:T(128)S(1)}, f32[8,1024]{1,0:T(8,128)S(1)}) all-reduce(f32[8]{0:T(128)S(1)} %reshape.217, f32[8,1024]{1,0:T(8,128)S(1)} %fusion.51), channel_id=1, replica_groups=mesh['dp'=32,'tensor'=16] {'tensor'}, use_global_device_ids=true, to_apply=%region_3.5 | all-reduce | flops 8200 | bytes 65600 | tf_op jit(solution)/shard_map/psum | solution.py:91
  344.7 4.2 %all-reduce.6.cloned.1.call-done = (f32[8,2048]{1,0:T(8,128)}, f32[512,1820]{0,1:T(8,128)}) async-done(((f32[8,2048]{1,0:T(8,128)}, f32[512,1820]{0,1:T(8,128)}), (f32[8,2048]{1,0:T(8,128)}, f32[512,1820]{0,1:T(8,128)})) %all-reduce.6.cloned.1.call-update) | async-done | bytes 3792912 | tf_op jit(solution)/shard_map/psum | solution.py:91
  349.0 0.8 multiply_convert_fusion.1
  349.7 1.0 fusion.48
  351.0 1.2 fusion.10
  352.3 0.7 copy.145
  353.0 1.3 fusion.8
  354.2 0.7 copy.146
  355.0 0.9 fusion.14
  355.9 0.8 fusion.5
  (55 shorter events, 3.0 us)
Async XLA Ops:
  7.2 56.0 %copy-start = (bf16[512,2,448]{0,2,1:T(8,128)(2,1)S(1)}, bf16[512,2,448]{0,2,1:T(8,128)(2,1)}, u32[]{:S(2)}) copy-start(bf16[512,2,448]{0,2,1:T(8,128)(2,1)} %param.26) | copy-start | bytes 2752516
  8.6 60.6 %all-to-all-start = ((s32[32,2,4]{2,1,0:T(2,128)}), s32[32,2,4]{2,1,0:T(2,128)S(1)}, u32[]{:S(2)}, u32[]{:S(2)}) async-start(s32[32,2,4]{2,1,0:T(2,128)} %stack.2), calls=%async_computation | async-start | bytes 65536 | tf_op jit(solution)/shard_map/all_to_all | solution.py:66
  22.3 326.7 %all-reduce.6.cloned.1.call-start = ((), (), s32[]{:S(2)}) async-start(), calls=%async_computation.1 | async-start | bytes 7602176 | tf_op jit(solution)/shard_map/psum | solution.py:91
  63.9 2.3 copy-start.1
  66.1 1.0 copy-start.6
  67.1 118.4 %copy-start.2 = (bf16[224,2048]{1,0:T(8,128)(2,1)S(1)}, bf16[224,2048]{1,0:T(8,128)(2,1)}, u32[]{:S(2)}) copy-start(bf16[224,2048]{1,0:T(8,128)(2,1)} %param.20) | copy-start | bytes 2752516
  186.4 0.7 copy-start.4
  186.4 30.0 %copy-start.5 = (s32[1,4]{1,0:T(1,128)S(1)}, s32[1,4]{1,0:T(1,128)}, u32[]{:S(2)}) copy-start(s32[1,4]{1,0:T(1,128)} %param.28) | copy-start | bytes 52
  186.4 59.8 %copy-start.7 = (s32[2]{0:T(128)S(1)}, s32[2]{0:T(128)}, u32[]{:S(2)}) copy-start(s32[2]{0:T(128)} %param.24) | copy-start | bytes 28
  186.4 60.0 %copy-start.3 = (bf16[224,1024]{1,0:T(8,128)(2,1)S(1)}, bf16[224,1024]{1,0:T(8,128)(2,1)}, u32[]{:S(2)}) copy-start(bf16[224,1024]{1,0:T(8,128)(2,1)} %param.21) | copy-start | bytes 1376260
Sparse Core Ops, SparseCore 0:
  186.5 162.3 all-reduce.5
